TPU v7x, 32 devices: a whole 2x2x4 slice. The times are simulated.
32 devices in a mesh: dp: 4 (over x, core), head: 8 (over z, y).
Axes of the slice: x: 2, y: 2, z: 4, core: 2. Of those that a mesh axis runs over, the one named last changes fastest.
Arguments:
- query_nope: bfloat16 [2, 512, 2048], P(None, ('dp', 'head')), may hold values from -12 to 12
- query_rope: bfloat16 [2, 512, 1024], P(None, ('dp', 'head')), may hold values from -640 to 640
- key_up: bfloat16 [2, 16, 128, 512], P(None, 'dp'), may hold values from -0.5 to 0.5
- value_up: bfloat16 [2, 16, 512, 128], P(None, 'dp'), may hold values from -0.25 to 0.25
- pool_latent: bfloat16 [2, 8, 128, 512], P(None, 'head'), may hold values from -6 to 6
- pool_rope: bfloat16 [2, 8, 64, 128], P(None, 'head'), may hold values from -8 to 8
- block_table: int32 [2, 6], replicated, may hold values from 0 to 7, as said below
- suffix_latent: bfloat16 [2, 512, 128, 512], P(None, ('dp', 'head')), may hold values from -8 to 8
- suffix_rope: bfloat16 [2, 512, 64, 128], P(None, ('dp', 'head')), may hold values from -8 to 8
- lengths: int32 [512], P(('dp', 'head')), may hold values from 1 to 128, as said below
Outputs:
- attention: bfloat16 [2, 512, 2048], P(None, ('dp', 'head'))
Inputs may be any that keep to these rules, and one draw needn't show every extreme that they name: `block_table`: each row names 6 different slots. `lengths`: among the 16 sequences of every device at least one has length 128.
All inputs are finite; a program needn't handle non-finite values.
Results may differ from a plain program's by a relative error of at most 0.0087.
Values may be sent and summed in bfloat16 or wider, within the bound.
A program may use at most 128 MiB of HBM per device.

v0:
```python
import jax
import jax.numpy as jnp
from jax import lax
from jax.sharding import PartitionSpec as P

HEADS = 16
NOPE = 128
ROPE = 64
VDIM = 128


def fold_blocks(state_now, latent_piece, rope_piece, usable, q_latent, q_rotary):
    running_max, running_sum, gathered = state_now
    scores = jnp.einsum("shc,ktc->shkt", q_latent, latent_piece, preferred_element_type=jnp.float32)
    scores = scores + jnp.einsum(
        "shr,krt->shkt", q_rotary, rope_piece, preferred_element_type=jnp.float32
    )
    scores = scores * (NOPE + ROPE) ** (-0.5)
    keep_mask = usable[None, None, :, None] > 0
    piece_top = jnp.max(jnp.where(keep_mask, scores, -jnp.inf), axis=(2, 3))
    new_max = jnp.maximum(running_max, piece_top)
    weights = jnp.where(keep_mask, jnp.exp(scores - new_max[..., None, None]), 0.0)
    factor = jnp.exp(running_max - new_max)
    running_sum = running_sum * factor + jnp.sum(weights, axis=(2, 3))
    update = jnp.einsum(
        "shkt,ktc->shc",
        weights.astype(jnp.bfloat16),
        latent_piece,
        preferred_element_type=jnp.float32,
    )
    gathered = gathered * factor[..., None] + update
    return (new_max, running_sum, gathered)


def on_device(
    query_nope,
    query_rope,
    key_up,
    value_up,
    pool_latent,
    pool_rope,
    block_table,
    suffix_latent,
    suffix_rope,
    lengths,
):
    layer_count = query_nope.shape[0]
    sequences = query_nope.shape[1]
    pool_size = pool_latent.shape[1] * lax.axis_size("head")
    suffix_len = suffix_latent.shape[2]
    results = []
    for layer_index in range(layer_count):
        q_heads = query_nope[layer_index].reshape(sequences, HEADS, NOPE)
        q_rotary = query_rope[layer_index].reshape(sequences, HEADS, ROPE)
        held_queries = lax.all_to_all(q_heads, "dp", split_axis=1, concat_axis=0, tiled=True)
        held_latent = jnp.einsum(
            "shd,hdc->shc", held_queries, key_up[layer_index], preferred_element_type=jnp.float32
        ).astype(jnp.bfloat16)
        q_latent = lax.all_to_all(held_latent, "dp", split_axis=0, concat_axis=1, tiled=True)
        own_latent = suffix_latent[layer_index]
        own_rope = suffix_rope[layer_index]
        own_scores = jnp.einsum(
            "shc,stc->sht", q_latent, own_latent, preferred_element_type=jnp.float32
        )
        own_scores = own_scores + jnp.einsum(
            "shr,srt->sht", q_rotary, own_rope, preferred_element_type=jnp.float32
        )
        own_scores = own_scores * (NOPE + ROPE) ** (-0.5)
        live_mask = (jnp.arange(suffix_len)[None, :] < lengths[:, None])[:, None, :]
        start_max = jnp.max(jnp.where(live_mask, own_scores, -jnp.inf), axis=2)
        own_weights = jnp.where(live_mask, jnp.exp(own_scores - start_max[..., None]), 0.0)
        start_sum = jnp.sum(own_weights, axis=2)
        start_gathered = jnp.einsum(
            "sht,stc->shc",
            own_weights.astype(jnp.bfloat16),
            own_latent,
            preferred_element_type=jnp.float32,
        )
        initial = (start_max, start_sum, start_gathered)
        slot_ids = jnp.arange(pool_size, dtype=jnp.int32)
        usable_slots = jnp.sum(
            (block_table[layer_index][:, None] == slot_ids[None, :]).astype(jnp.float32), axis=0
        )
        final_state = fold_blocks(
            initial,
            lax.all_gather(pool_latent[layer_index], "head", axis=0, tiled=True),
            lax.all_gather(pool_rope[layer_index], "head", axis=0, tiled=True),
            usable_slots,
            q_latent,
            q_rotary,
        )
        final_max, final_sum, final_gathered = final_state
        latent_out = (final_gathered / final_sum[..., None]).astype(jnp.bfloat16)
        held_outputs = lax.all_to_all(latent_out, "dp", split_axis=1, concat_axis=0, tiled=True)
        held_values = jnp.einsum(
            "shc,hcv->shv", held_outputs, value_up[layer_index], preferred_element_type=jnp.float32
        ).astype(jnp.bfloat16)
        expanded = lax.all_to_all(held_values, "dp", split_axis=0, concat_axis=1, tiled=True)
        results.append(expanded.reshape(sequences, HEADS * VDIM))
    return jnp.stack(results)


def solution(mesh):
    return jax.shard_map(
        on_device,
        mesh=mesh,
        in_specs=(
            P(None, ("dp", "head"), None),
            P(None, ("dp", "head"), None),
            P(None, "dp", None, None),
            P(None, "dp", None, None),
            P(None, "head", None, None),
            P(None, "head", None, None),
            P(),
            P(None, ("dp", "head"), None, None),
            P(None, ("dp", "head"), None, None),
            P(("dp", "head")),
        ),
        out_specs=P(None, ("dp", "head"), None),
        check_vma=False,
    )
```

profile of v0, /device:TPU:0, one launch (start us, length us, event | category | flops | bytes accessed | tf_op | source)
XLA Modules:
  0.0 160.8 jit_solution(8686443954345640827)
XLA Ops:
  6.5 1.8 %fusion.108 = (bf16[1,1,128,512]{3,2,1,0:T(8,128)(2,1)}, bf16[1,1,128,512]{3,2,1,0:T(8,128)(2,1)}) fusion(bf16[2,1,128,512]{3,2,1,0:T(8,128)(2,1)} %param.14), kind=kLoop, calls=%fused_computation.114 | loop fusion | bytes 524288 | tf_op jit(solution)/shard_map/slice | solution.py:86
  8.3 0.9 slice_bitcast_fusion.1
  9.2 0.6 copy.71
  9.9 4.2 %all-to-all-start.4 = ((bf16[16,16,128]{2,0,1:T(8,128)(2,1)}), bf16[16,16,128]{2,0,1:T(8,128)(2,1)S(1)}, u32[]{:S(2)}, u32[]{:S(2)}) async-start(bf16[16,16,128]{2,0,1:T(8,128)(2,1)} %copy.71), calls=%async_computation.4 | async-start | bytes 131072 | tf_op jit(solution)/shard_map/all_to_all | solution.py:55
  14.1 0.7 all-gather.7.cloned.1.call-update
  14.9 0.8 fusion.109
  15.6 0.1 reshape.86
  15.8 0.1 reshape_squeeze.15
  15.9 0.1 reshape_squeeze.13
  16.0 0.1 reshape.81
  16.1 0.8 slice_bitcast_fusion.3
  16.9 0.1 convert_reduce_fusion
  17.0 0.7 fusion.110
  17.7 31.9 %all-gather.3 = bf16[8,1,64,128]{3,2,1,0:T(8,128)(2,1)S(1)} all-gather(bf16[1,1,64,128]{3,2,1,0:T(8,128)(2,1)S(1)} %get-tuple-element.18), channel_id=5, replica_groups=mesh['dp'=4,'head'=8] {'head'}, dimensions={0}, use_global_device_ids=true | all-gather | bytes 147456 | tf_op jit(solution)/shard_map/all_gather | solution.py:87
  49.6 0.7 iota_compare_fusion
  50.3 0.6 copy.63
  51.0 1.1 fusion.84
  52.1 1.1 fusion.81
  53.2 0.1 convert_reduce_fusion.1
  53.3 30.6 %all-gather.1 = bf16[8,1,64,128]{3,2,1,0:T(8,128)(2,1)S(1)} all-gather(bf16[1,1,64,128]{3,2,1,0:T(8,128)(2,1)S(1)} %get-tuple-element.17), channel_id=3, replica_groups=mesh['dp'=4,'head'=8] {'head'}, dimensions={0}, use_global_device_ids=true | all-gather | bytes 147456 | tf_op jit(solution)/shard_map/all_gather | solution.py:87
  84.0 3.3 %all-to-all-start = ((bf16[16,16,128]{2,0,1:T(8,128)(2,1)}), bf16[16,16,128]{2,0,1:T(8,128)(2,1)S(1)}, u32[]{:S(2)}, u32[]{:S(2)}) async-start(bf16[16,16,128]{2,0,1:T(8,128)(2,1)} %copy.63), calls=%async_computation | async-start | bytes 131072 | tf_op jit(solution)/shard_map/all_to_all | solution.py:55
  87.3 1.3 fusion.39
  88.5 0.9 copy.73
  89.4 1.9 %all-to-all-done = bf16[16,16,128]{2,0,1:T(8,128)(2,1)S(1)} async-done(((bf16[16,16,128]{2,0,1:T(8,128)(2,1)}), bf16[16,16,128]{2,0,1:T(8,128)(2,1)S(1)}, u32[]{:S(2)}, u32[]{:S(2)}) %all-to-all-start) | async-done | bytes 65568 | tf_op jit(solution)/shard_map/all_to_all | solution.py:55
  91.4 3.4 %all-to-all-start.5 = ((bf16[64,4,512]{2,1,0:T(4,128)(2,1)}), bf16[64,4,512]{2,1,0:T(4,128)(2,1)S(1)}, u32[]{:S(2)}, u32[]{:S(2)}) async-start(bf16[64,4,512]{2,1,0:T(4,128)(2,1)} %copy.73), calls=%async_computation.5 | async-start | bytes 524288 | tf_op jit(solution)/shard_map/all_to_all | solution.py:59
  94.8 0.2 fusion.38
  95.0 0.9 copy.65
  95.9 4.8 %all-to-all-done.5 = bf16[64,4,512]{2,1,0:T(4,128)(2,1)S(1)} async-done(((bf16[64,4,512]{2,1,0:T(4,128)(2,1)}), bf16[64,4,512]{2,1,0:T(4,128)(2,1)S(1)}, u32[]{:S(2)}, u32[]{:S(2)}) %all-to-all-start.5) | async-done | bytes 262176 | tf_op jit(solution)/shard_map/all_to_all | solution.py:59
  100.7 3.4 %all-to-all-start.1 = ((bf16[64,4,512]{2,1,0:T(4,128)(2,1)}), bf16[64,4,512]{2,1,0:T(4,128)(2,1)S(1)}, u32[]{:S(2)}, u32[]{:S(2)}) async-start(bf16[64,4,512]{2,1,0:T(4,128)(2,1)} %copy.65), calls=%async_computation.1 | async-start | bytes 524288 | tf_op jit(solution)/shard_map/all_to_all | solution.py:59
  104.2 0.1 copy.89
  104.3 0.1 reshape.84
  104.4 0.1 all_to_all.122
  104.4 5.7 %all-to-all-done.1 = bf16[64,4,512]{2,1,0:T(4,128)(2,1)S(1)} async-done(((bf16[64,4,512]{2,1,0:T(4,128)(2,1)}), bf16[64,4,512]{2,1,0:T(4,128)(2,1)S(1)}, u32[]{:S(2)}, u32[]{:S(2)}) %all-to-all-start.1) | async-done | bytes 262176 | tf_op jit(solution)/shard_map/all_to_all | solution.py:59
  110.1 0.1 copy.90
  110.2 0.1 all_to_all.107
  110.3 0.1 reshape.79
  110.4 2.3 %select_reduce_fusion.3 = (f32[16,16]{1,0:T(8,128)S(1)}, f32[16,16,128]{2,1,0:T(8,128)S(1)}) fusion(pred[16,128]{1,0:T(8,128)(4,1)S(1)} %iota_compare_fusion, f32[16,16,128]{2,1,0:T(8,128)S(1)} %fusion.84, bf16[16,16,512]{2,1,0:T(8,128)(2,1)S(1)} %all_to_all.107, bf16[2,16,128,512]{3,2,1,0:T(8,128)(2,1)} %param.17), kind=kOutput, calls=%fused_computation.82 | convolution fusion | flops 33685248 | bytes 2624512 | tf_op jit(solution)/shard_map/shc,stc->sht/dot_general | solution.py:62
  112.7 2.3 %fusion.90 = (f32[16,16]{1,0:T(8,128)S(1)}, f32[16,16]{1,0:T(8,128)S(1)}, f32[16,16,128]{2,1,0:T(8,128)S(1)}) fusion(f32[16,16,128]{2,1,0:T(8,128)S(1)} %get-tuple-element.22, f32[16,16]{1,0:T(8,128)S(1)} %get-tuple-element.21, pred[16,128]{1,0:T(8,128)(4,1)S(1)} %iota_compare_fusion, f32[16,16,128]{2,1,0:T(8,128)S(1)} %fusion.81, ...), kind=kOutput, calls=%fused_computation.83 | convolution fusion | flops 33783296 | bytes 2757632 | tf_op jit(solution)/shard_map/shc,stc->sht/dot_general | solution.py:62
  115.0 0.2 fusion.92
  115.3 1.8 %fusion.55 = f32[16,16,8,128]{3,1,2,0:T(8,128)S(1)} fusion(bf16[8,1,128,512]{3,2,1,0:T(8,128)(2,1)} %all-gather.9.cloned.1.call-done, bf16[16,16,512,1]{2,1,0,3:T(8,128)(2,1)S(1)} %reshape.84), kind=kOutput, calls=%fused_computation.39 | convolution fusion | flops 268435456 | bytes 2359296 | tf_op jit(solution)/shard_map/shc,ktc->shkt/dot_general | solution.py:14
  117.2 0.4 select_reduce_fusion
  117.5 0.3 fusion.62
  117.9 0.5 convolution_bitcast_fusion
  118.4 0.5 fusion.35
  118.8 0.9 copy.75
  119.7 3.4 %all-to-all-start.6 = ((bf16[16,16,512]{2,0,1:T(8,128)(2,1)}), bf16[16,16,512]{2,0,1:T(8,128)(2,1)S(1)}, u32[]{:S(2)}, u32[]{:S(2)}) async-start(bf16[16,16,512]{2,0,1:T(8,128)(2,1)} %copy.75), calls=%async_computation.6 | async-start | bytes 524288 | tf_op jit(solution)/shard_map/all_to_all | solution.py:94
  123.2 1.8 %fusion.58 = f32[16,16,8,128]{3,1,2,0:T(8,128)S(1)} fusion(bf16[8,1,128,512]{3,2,1,0:T(8,128)(2,1)} %all-gather.7.cloned.1.call-done, bf16[16,16,512,1]{2,1,0,3:T(8,128)(2,1)S(1)} %reshape.79), kind=kOutput, calls=%fused_computation.42 | convolution fusion | flops 268435456 | bytes 2359296 | tf_op jit(solution)/shard_map/shc,ktc->shkt/dot_general | solution.py:14
  125.0 0.4 select_reduce_fusion.1
  125.4 0.3 fusion.60
  125.8 0.5 convolution_bitcast_fusion.1
  126.3 0.5 fusion.32
  126.7 0.9 copy.67
  127.6 1.5 all-to-all-done.6
  129.1 3.4 %all-to-all-start.2 = ((bf16[16,16,512]{2,0,1:T(8,128)(2,1)}), bf16[16,16,512]{2,0,1:T(8,128)(2,1)S(1)}, u32[]{:S(2)}, u32[]{:S(2)}) async-start(bf16[16,16,512]{2,0,1:T(8,128)(2,1)} %copy.67), calls=%async_computation.2 | async-start | bytes 524288 | tf_op jit(solution)/shard_map/all_to_all | solution.py:94
  132.5 0.2 fusion.53
  132.8 0.7 copy.77
  133.5 5.0 %all-to-all-done.2 = bf16[16,16,512]{2,0,1:T(8,128)(2,1)S(1)} async-done(((bf16[16,16,512]{2,0,1:T(8,128)(2,1)}), bf16[16,16,512]{2,0,1:T(8,128)(2,1)S(1)}, u32[]{:S(2)}, u32[]{:S(2)}) %all-to-all-start.2) | async-done | bytes 262176 | tf_op jit(solution)/shard_map/all_to_all | solution.py:94
  138.5 3.3 %all-to-all-start.7 = ((bf16[64,4,128]{2,1,0:T(4,128)(2,1)}), bf16[64,4,128]{2,1,0:T(4,128)(2,1)S(1)}, u32[]{:S(2)}, u32[]{:S(2)}) async-start(bf16[64,4,128]{2,1,0:T(4,128)(2,1)} %copy.77), calls=%async_computation.7 | async-start | bytes 131072 | tf_op jit(solution)/shard_map/all_to_all | solution.py:98
  141.8 0.2 fusion.52
  142.0 0.7 copy.69
  142.7 3.2 %all-to-all-done.7 = bf16[64,4,128]{2,1,0:T(4,128)(2,1)S(1)} async-done(((bf16[64,4,128]{2,1,0:T(4,128)(2,1)}), bf16[64,4,128]{2,1,0:T(4,128)(2,1)S(1)}, u32[]{:S(2)}, u32[]{:S(2)}) %all-to-all-start.7) | async-done | bytes 65568 | tf_op jit(solution)/shard_map/all_to_all | solution.py:98
  145.9 3.3 %all-to-all-start.3 = ((bf16[64,4,128]{2,1,0:T(4,128)(2,1)}), bf16[64,4,128]{2,1,0:T(4,128)(2,1)S(1)}, u32[]{:S(2)}, u32[]{:S(2)}) async-start(bf16[64,4,128]{2,1,0:T(4,128)(2,1)} %copy.69), calls=%async_computation.3 | async-start | bytes 131072 | tf_op jit(solution)/shard_map/all_to_all | solution.py:98
  149.2 4.0 %all-to-all-done.3 = bf16[64,4,128]{2,1,0:T(4,128)(2,1)S(1)} async-done(((bf16[64,4,128]{2,1,0:T(4,128)(2,1)}), bf16[64,4,128]{2,1,0:T(4,128)(2,1)S(1)}, u32[]{:S(2)}, u32[]{:S(2)}) %all-to-all-start.3) | async-done | bytes 65568 | tf_op jit(solution)/shard_map/all_to_all | solution.py:98
  153.3 0.7 pad_maximum_fusion
  (34 shorter events, 0.3 us)
Async XLA Ops:
  6.5 88.2 %copy-start.4 = (bf16[2,4,128,512]{3,2,1,0:T(8,128)(2,1)S(1)}, bf16[2,4,128,512]{3,2,1,0:T(8,128)(2,1)}, u32[]{:S(2)}) copy-start(bf16[2,4,128,512]{3,2,1,0:T(8,128)(2,1)} %param.12) | copy-start | bytes 3145732
  6.5 108.7 %all-gather.9.cloned.1.call-start = ((), (), s32[]{:S(2)}) async-start(), calls=%async_computation.9 | async-start | bytes 1179648 | tf_op jit(solution)/shard_map/all_gather | solution.py:86
  9.9 74.1 %all-to-all-start.4 = ((bf16[16,16,128]{2,0,1:T(8,128)(2,1)}), bf16[16,16,128]{2,0,1:T(8,128)(2,1)S(1)}, u32[]{:S(2)}, u32[]{:S(2)}) async-start(bf16[16,16,128]{2,0,1:T(8,128)(2,1)} %copy.71), calls=%async_computation.4 | async-start | bytes 131072 | tf_op jit(solution)/shard_map/all_to_all | solution.py:55
  14.1 109.0 %all-gather.7.cloned.1.call-start = ((), (), s32[]{:S(2)}) async-start(), calls=%async_computation.8 | async-start | bytes 1179648 | tf_op jit(solution)/shard_map/all_gather | solution.py:86
  84.0 7.4 %all-to-all-start = ((bf16[16,16,128]{2,0,1:T(8,128)(2,1)}), bf16[16,16,128]{2,0,1:T(8,128)(2,1)S(1)}, u32[]{:S(2)}, u32[]{:S(2)}) async-start(bf16[16,16,128]{2,0,1:T(8,128)(2,1)} %copy.63), calls=%async_computation | async-start | bytes 131072 | tf_op jit(solution)/shard_map/all_to_all | solution.py:55
  91.4 9.4 %all-to-all-start.5 = ((bf16[64,4,512]{2,1,0:T(4,128)(2,1)}), bf16[64,4,512]{2,1,0:T(4,128)(2,1)S(1)}, u32[]{:S(2)}, u32[]{:S(2)}) async-start(bf16[64,4,512]{2,1,0:T(4,128)(2,1)} %copy.73), calls=%async_computation.5 | async-start | bytes 524288 | tf_op jit(solution)/shard_map/all_to_all | solution.py:59
  100.7 9.4 %all-to-all-start.1 = ((bf16[64,4,512]{2,1,0:T(4,128)(2,1)}), bf16[64,4,512]{2,1,0:T(4,128)(2,1)S(1)}, u32[]{:S(2)}, u32[]{:S(2)}) async-start(bf16[64,4,512]{2,1,0:T(4,128)(2,1)} %copy.65), calls=%async_computation.1 | async-start | bytes 524288 | tf_op jit(solution)/shard_map/all_to_all | solution.py:59
  115.3 2.6 %copy-start.3 = (bf16[8,1,128,512]{3,2,1,0:T(8,128)(2,1)S(1)}, bf16[8,1,128,512]{3,2,1,0:T(8,128)(2,1)}, u32[]{:S(2)}) copy-start(bf16[8,1,128,512]{3,2,1,0:T(8,128)(2,1)} %all-gather.9.cloned.1.call-done) | copy-start | bytes 3145732
  115.3 3.1 %copy-start = (bf16[2,16,128,512]{3,2,1,0:T(8,128)(2,1)S(1)}, bf16[2,16,128,512]{3,2,1,0:T(8,128)(2,1)}, u32[]{:S(2)}) copy-start(bf16[2,16,128,512]{3,2,1,0:T(8,128)(2,1)} %param.17) | copy-start | bytes 12582916
  119.7 9.4 %all-to-all-start.6 = ((bf16[16,16,512]{2,0,1:T(8,128)(2,1)}), bf16[16,16,512]{2,0,1:T(8,128)(2,1)S(1)}, u32[]{:S(2)}, u32[]{:S(2)}) async-start(bf16[16,16,512]{2,0,1:T(8,128)(2,1)} %copy.75), calls=%async_computation.6 | async-start | bytes 524288 | tf_op jit(solution)/shard_map/all_to_all | solution.py:94
  123.2 2.6 %copy-start.2 = (bf16[8,1,128,512]{3,2,1,0:T(8,128)(2,1)S(1)}, bf16[8,1,128,512]{3,2,1,0:T(8,128)(2,1)}, u32[]{:S(2)}) copy-start(bf16[8,1,128,512]{3,2,1,0:T(8,128)(2,1)} %all-gather.7.cloned.1.call-done) | copy-start | bytes 3145732
  123.2 3.1 %copy-start.1 = (bf16[2,16,128,512]{3,2,1,0:T(8,128)(2,1)S(1)}, bf16[2,16,128,512]{3,2,1,0:T(8,128)(2,1)}, u32[]{:S(2)}) copy-start(bf16[2,16,128,512]{3,2,1,0:T(8,128)(2,1)} %param.17) | copy-start | bytes 12582916
  125.8 6.8 %copy-start.5 = (bf16[2,4,512,128]{3,2,1,0:T(8,128)(2,1)S(1)}, bf16[2,4,512,128]{3,2,1,0:T(8,128)(2,1)}, u32[]{:S(2)}) copy-start(bf16[2,4,512,128]{3,2,1,0:T(8,128)(2,1)} %param.13) | copy-start | bytes 3145732
  129.1 9.4 %all-to-all-start.2 = ((bf16[16,16,512]{2,0,1:T(8,128)(2,1)}), bf16[16,16,512]{2,0,1:T(8,128)(2,1)S(1)}, u32[]{:S(2)}, u32[]{:S(2)}) async-start(bf16[16,16,512]{2,0,1:T(8,128)(2,1)} %copy.67), calls=%async_computation.2 | async-start | bytes 524288 | tf_op jit(solution)/shard_map/all_to_all | solution.py:94
  138.5 7.4 %all-to-all-start.7 = ((bf16[64,4,128]{2,1,0:T(4,128)(2,1)}), bf16[64,4,128]{2,1,0:T(4,128)(2,1)S(1)}, u32[]{:S(2)}, u32[]{:S(2)}) async-start(bf16[64,4,128]{2,1,0:T(4,128)(2,1)} %copy.77), calls=%async_computation.7 | async-start | bytes 131072 | tf_op jit(solution)/shard_map/all_to_all | solution.py:98
  145.9 7.4 %all-to-all-start.3 = ((bf16[64,4,128]{2,1,0:T(4,128)(2,1)}), bf16[64,4,128]{2,1,0:T(4,128)(2,1)S(1)}, u32[]{:S(2)}, u32[]{:S(2)}) async-start(bf16[64,4,128]{2,1,0:T(4,128)(2,1)} %copy.69), calls=%async_computation.3 | async-start | bytes 131072 | tf_op jit(solution)/shard_map/all_to_all | solution.py:98
Sparse Core Ops, SparseCore 0:
  9.5 43.0 all-gather.8
  54.7 39.3 all-gather.6
where the time goes:
time: 162 us; the launch traced here: 161 us
  blocking collectives  62.5 us (39%)
  starting transfers between devices  27.7 us (17%)
  waiting for transfers between devices  26.9 us (17%)
  matrix products  15.1 us (9%)
  between operations  13.8 us (9%)
  local copies, waits for them, and re-layouts  12.3 us (8%)
  other arithmetic  2.49 us (2%)
    all_gather x2, blocking collectives, on_device(): lax.all_gather(pool_rope[layer_index], 'head', axis=0, tiled=True)  62.5 us
    all_to_all x2, waiting for transfers between devices, on_device(): lax.all_to_all(held_latent, 'dp', split_axis=0, concat_axis=1, tiled=True)  10.5 us
    all_to_all x2, starting transfers between devices, on_device(): lax.all_to_all(q_heads, 'dp', split_axis=1, concat_axis=0, tiled=True)  7.52 us
    all_to_all x2, waiting for transfers between devices, on_device(): lax.all_to_all(held_values, 'dp', split_axis=0, concat_axis=1, tiled=True)  7.17 us
    all_to_all x2, starting transfers between devices, on_device(): lax.all_to_all(held_latent, 'dp', split_axis=0, concat_axis=1, tiled=True)  6.81 us
    all_to_all x2, starting transfers between devices, on_device(): lax.all_to_all(latent_out, 'dp', split_axis=1, concat_axis=0, tiled=True)  6.81 us
    all_to_all x2, starting transfers between devices, on_device(): lax.all_to_all(held_values, 'dp', split_axis=0, concat_axis=1, tiled=True)  6.57 us
    all_to_all x2, waiting for transfers between devices, on_device(): lax.all_to_all(latent_out, 'dp', split_axis=1, concat_axis=0, tiled=True)  6.54 us
  transfers between devices with their start and end apart: 10, of which 7 were waited for; matrix products, arithmetic and copies ran while one was open for 17% of the time, Pallas kernels for 0%

commit v1 on v0

v1 whole, which is shorter than its diff:
```python
import functools

import jax
import jax.numpy as jnp
from jax import lax
from jax.experimental import pallas as pl
from jax.experimental.pallas import tpu as pltpu
from jax.sharding import PartitionSpec as P

HEADS = 16
NOPE = 128
ROPE = 64
VDIM = 128
SCALE = (NOPE + ROPE) ** (-0.5)
MESH = pl.DeviceIdType.MESH
F32 = jnp.float32
BF16 = jnp.bfloat16
NT = (((1,), (1,)), ((), ()))


def dot(a, b):
    return jnp.dot(a, b, preferred_element_type=F32)


def dot_nt(a, b):
    return lax.dot_general(a, b, NT, preferred_element_type=F32)


def kernel(dims, *refs):
    (layers, seqs, groups, heads_dev, rank, blk, suf, per, ring, nblk, chunk) = dims
    it = iter(refs)

    def take(count):
        return [next(it) for _ in range(count)]

    qn, qr, ku, vu, pool_lat, pool_rope, table, suf_lat, suf_rope, lengths = take(10)
    (out,) = take(1)
    qr_v, ku_v, vu_v, sl_v, sr_v = take(5)
    plat = take(layers)
    prope = take(layers)
    hq, scr, qls, qlat, qrf, qrot, m_ref, l_ref, acc, s_ref, kbuf, rbuf, los, lr, hvs = take(15)
    (
        loc_sem, pown_sem, own_sem,
        q_ss, q_rs, ql_ss, ql_rs, lo_ss, lo_rs, hv_ss, hv_rs,
        z_ss, z_rs, y_ss, y_rs, c_ss, c_rs,
    ) = take(17)

    dp = lax.axis_index("dp")
    hd = lax.axis_index("head")
    core = lax.rem(dp, 2)
    partner = dp + 1 - 2 * core
    za, yb = hd // 2, lax.rem(hd, 2)
    outer = ring // 2
    wide = heads_dev * NOPE
    rows_g = seqs * heads_dev
    rows = groups * rows_g
    quad = 16 // heads_dev
    nquads = seqs // quad

    local = []

    def fetch(src, dst, sem):
        cp = pltpu.make_async_copy(src, dst, sem)
        cp.start()
        return cp

    def own_q(l):
        return pltpu.make_async_copy(
            qn.at[l, :, pl.ds(pl.multiple_of(dp * wide, 128), wide)], hq.at[l, dp], own_sem.at[0, l]
        )

    for l in range(layers):
        own_q(l).start()
    c_ku = [fetch(ku.at[l], ku_v.at[l], loc_sem.at[0, l]) for l in range(layers)]
    c_qr = fetch(qr, qr_v, loc_sem.at[1, 0])
    c_sl = [fetch(suf_lat.at[l], sl_v.at[l], loc_sem.at[2, l]) for l in range(layers)]
    c_sr = [fetch(suf_rope.at[l], sr_v.at[l], loc_sem.at[3, l]) for l in range(layers)]
    c_po = []
    for l in range(layers):
        mine = pl.ds(hd * per, per)
        c_po.append(fetch(pool_lat.at[l], plat[l].at[mine], pown_sem.at[0, l]))
        c_po.append(fetch(pool_rope.at[l], prope[l].at[mine], pown_sem.at[1, l]))
    c_vu = [fetch(vu.at[l], vu_v.at[l], loc_sem.at[4, l]) for l in range(layers)]

    barrier = pltpu.get_barrier_semaphore()

    def greet(d, h):
        pl.semaphore_signal(barrier, inc=1, device_id=(d, h), device_id_type=MESH)

    for i in range(1, groups):
        greet(lax.rem(dp + i, groups), hd)
    for_z = lambda i: lax.rem(za + i, outer)

    def greet_z(i, carry):
        greet(dp, for_z(i) * 2 + yb)
        return carry

    lax.fori_loop(1, outer, greet_z, 0)
    greet(dp, za * 2 + 1 - yb)
    pl.semaphore_wait(barrier, (groups - 1) + (outer - 1) + 1)

    def remote(src, dst, ss, rs, d, h):
        return pltpu.make_async_remote_copy(
            src_ref=src, dst_ref=dst, send_sem=ss, recv_sem=rs, device_id=(d, h), device_id_type=MESH
        )

    def peer(i):
        return lax.rem(dp + i, groups)

    def send_q(l, i):
        j = peer(i)
        return remote(
            qn.at[l, :, pl.ds(pl.multiple_of(j * wide, 128), wide)], hq.at[l, dp],
            q_ss.at[l, j], q_rs.at[l, dp], j, hd,
        )

    def recv_q(l, i):
        j = peer(i)
        return remote(hq.at[l, j], hq.at[l, j], q_ss.at[l, j], q_rs.at[l, j], j, hd)

    def pair(sends, buf, ss, rs):
        def send(l, i):
            j = peer(i)
            return remote(sends.at[l, j], buf.at[l, dp], ss.at[l, j], rs.at[l, dp], j, hd)

        def recv(l, i):
            j = peer(i)
            return remote(sends.at[l, j], buf.at[l, j], ss.at[l, j], rs.at[l, j], j, hd)

        return send, recv

    send_ql, recv_ql = pair(qls, qlat, ql_ss, ql_rs)
    send_lo, recv_lo = pair(los, lr, lo_ss, lo_rs)

    def cols(j):
        return pl.ds(pl.multiple_of(j * heads_dev * VDIM, 128), heads_dev * VDIM)

    def send_hv(l, i):
        j = peer(i)
        return remote(hvs.at[l, j], out.at[l, :, cols(dp)], hv_ss.at[l, j], hv_rs.at[l, dp], j, hd)

    def recv_hv(l, i):
        j = peer(i)
        return remote(hvs.at[l, j], out.at[l, :, cols(j)], hv_ss.at[l, j], hv_rs.at[l, j], j, hd)

    def half(kind, c):
        size = (blk if kind == 0 else ROPE) // 2
        return pl.ds(pl.multiple_of(c * size, 16), size)

    def pool_at(l, kind, slot, c):
        buf = (plat if kind == 0 else prope)[l]
        return buf.at[pl.ds(slot * per, per), half(kind, c)]

    def own_piece(l, kind):
        return (pool_lat if kind == 0 else pool_rope).at[l, :, half(kind, core)]

    def send_z(l, kind, i):
        to = for_z(i)
        return remote(
            own_piece(l, kind), pool_at(l, kind, hd, core),
            z_ss.at[l, kind, to], z_rs.at[l, kind, za], dp, to * 2 + yb,
        )

    def recv_z(l, kind, i):
        frm = for_z(i)
        return remote(
            own_piece(l, kind), pool_at(l, kind, frm * 2 + yb, core),
            z_ss.at[l, kind, frm], z_rs.at[l, kind, frm], dp, frm * 2 + yb,
        )

    def send_y(l, kind, a, src):
        return remote(
            src, pool_at(l, kind, a * 2 + yb, core),
            y_ss.at[l, kind, a], y_rs.at[l, kind, a], dp, za * 2 + 1 - yb,
        )

    def recv_y(l, kind, a):
        return remote(
            own_piece(l, kind), pool_at(l, kind, a * 2 + 1 - yb, core),
            y_ss.at[l, kind, a], y_rs.at[l, kind, a], dp, za * 2 + 1 - yb,
        )

    def send_c(l, kind, slot):
        piece = pool_at(l, kind, slot, core)
        return remote(piece, piece, c_ss.at[l, kind, slot], c_rs.at[l, kind, slot], partner, hd)

    def recv_c(l, kind, slot):
        piece = pool_at(l, kind, slot, 1 - core)
        return remote(piece, piece, c_ss.at[l, kind, slot], c_rs.at[l, kind, slot], partner, hd)

    def loop(low, high, body):
        def step(i, carry):
            body(i)
            return carry

        lax.fori_loop(low, high, step, 0)

    for l in range(layers):
        for i in range(1, groups):
            send_q(l, i).start()
    for l in range(layers):
        for kind in range(2):
            send_y(l, kind, za, own_piece(l, kind)).start()

        def first(i):
            for kind in range(2):
                send_z(l, kind, i).start()

        loop(1, outer, first)

    def forward_z(l):
        def body(i):
            for kind in range(2):
                recv_z(l, kind, i).wait_recv()
                a = for_z(i)
                send_y(l, kind, a, pool_at(l, kind, a * 2 + yb, core)).start()
                send_c(l, kind, a * 2 + yb).start()

        loop(1, outer, body)

    def forward_y(l):
        def body(i):
            for kind in range(2):
                a = for_z(i)
                recv_y(l, kind, a).wait_recv()
                send_c(l, kind, a * 2 + 1 - yb).start()

        loop(0, outer, body)

    def others(body):
        loop(1, ring, lambda i: body(lax.rem(hd + i, ring)))

    def gather_c(l):
        def body(slot):
            for kind in range(2):
                recv_c(l, kind, slot).wait_recv()

        others(body)

    c_qr.wait()
    for l in range(layers):
        for g in range(groups):
            for h in range(heads_dev):
                at = (g * heads_dev + h) * ROPE
                piece = qr_v[l, :, (at // 128) * 128 : (at // 128 + 1) * 128].astype(F32)
                if at % 128:
                    piece = pltpu.roll(piece, 128 - at % 128, 1)
                qrf[pl.ds(g * rows_g + h, seqs, stride=heads_dev), :] = piece
        qrot[l] = qrf[...].astype(BF16)

    def absorb(l):
        own_q(l).wait()
        for i in range(1, groups):
            recv_q(l, i).wait_recv()
        c_ku[l].wait()
        for h in range(heads_dev):
            x = jnp.concatenate([hq[l, g, :, h * NOPE : (h + 1) * NOPE] for g in range(groups)], axis=0)
            r = dot(x, ku_v[l, h])
            for c in range(rank // 128):
                scr[c, pl.ds(h, groups * seqs, stride=heads_dev), :] = r[:, c * 128 : (c + 1) * 128]
        for g in range(groups):
            for c in range(rank // 128):
                qls[l, g, :, c * 128 : (c + 1) * 128] = scr[c, g * rows_g : (g + 1) * rows_g, :].astype(BF16)
        for i in range(1, groups):
            send_ql(l, i).start()
        qlat[l, dp] = qls[l, dp]

    def suffix(l):
        c_sl[l].wait()
        c_sr[l].wait()
        for i in range(1, groups):
            recv_ql(l, i).wait_recv()
        r_id = lax.broadcasted_iota(jnp.int32, (groups * 16, suf), 0)
        lane = lax.broadcasted_iota(jnp.int32, (groups * 16, suf), 1)
        row_seq = lax.rem(r_id // heads_dev, quad)
        for k in range(nquads):
            q = jnp.concatenate([qlat[l, g, k * 16 : (k + 1) * 16, :] for g in range(groups)], axis=0)
            qro = jnp.concatenate(
                [qrot[l, g * rows_g + k * 16 : g * rows_g + (k + 1) * 16, :] for g in range(groups)], axis=0
            )[:, :ROPE]
            keys = sl_v[l, k * quad : (k + 1) * quad].reshape(quad * suf, rank)
            turn = jnp.concatenate([sr_v[l, k * quad + u] for u in range(quad)], axis=1)
            s = (dot_nt(q, keys) + dot(qro, turn)) * SCALE
            live = jnp.concatenate(
                [(row_seq == u) & (lane < lengths[k * quad + u]) for u in range(quad)], axis=1
            )
            s = jnp.where(live, s, -jnp.inf)
            top = jnp.max(s, axis=1, keepdims=True)
            w = jnp.exp(s - top)
            tot = jnp.sum(w, axis=1, keepdims=True)
            o = dot(w.astype(BF16), keys)
            for g in range(groups):
                at = slice(g * rows_g + k * 16, g * rows_g + (k + 1) * 16)
                m_ref[l, at, :] = top[g * 16 : (g + 1) * 16]
                l_ref[l, at, :] = tot[g * 16 : (g + 1) * 16]
                acc[l, at, :] = o[g * 16 : (g + 1) * 16]

    def prefix(l):
        def some(b):
            for j in range(chunk):
                slot = table[l, b * chunk + j]
                kbuf[j * blk : (j + 1) * blk, :] = plat[l][slot]
                rbuf[:, j * blk : (j + 1) * blk] = prope[l][slot]
            q = qlat[l].reshape(rows, rank)
            s_ref[...] = (dot_nt(q, kbuf[...]) + dot(qrot[l][:, :ROPE], rbuf[...])) * SCALE
            old = m_ref[l]
            top = jnp.maximum(old, jnp.max(s_ref[...], axis=1, keepdims=True))
            w = jnp.exp(s_ref[...] - top)
            fac = jnp.exp(old - top)
            l_ref[l] = l_ref[l] * fac + jnp.sum(w, axis=1, keepdims=True)
            m_ref[l] = top
            acc[l] = acc[l] * fac + dot(w.astype(BF16), kbuf[...])

        if nblk == chunk:
            some(0)
        else:
            loop(0, nblk // chunk, some)
        res = acc[l] / l_ref[l]
        for c in range(rank // 128):
            scr[c] = res[:, c * 128 : (c + 1) * 128]
        for g in range(groups):
            for h in range(heads_dev):
                for c in range(rank // 128):
                    los[l, g, h * seqs : (h + 1) * seqs, c * 128 : (c + 1) * 128] = scr[
                        c, pl.ds(g * rows_g + h, seqs, stride=heads_dev), :
                    ].astype(BF16)
        for i in range(1, groups):
            send_lo(l, i).start()
        lr[l, dp] = los[l, dp]

    def own_out(l):
        return pltpu.make_async_copy(hvs.at[l, dp], out.at[l, :, cols(dp)], own_sem.at[1, l])

    def expand(l):
        c_vu[l].wait()
        for i in range(1, groups):
            recv_lo(l, i).wait_recv()
        for h in range(heads_dev):
            x = jnp.concatenate([lr[l, g, h * seqs : (h + 1) * seqs, :] for g in range(groups)], axis=0)
            v = dot(x, vu_v[l, h]).astype(BF16)
            for g in range(groups):
                hvs[l, g, :, h * VDIM : (h + 1) * VDIM] = v[g * seqs : (g + 1) * seqs]
        for i in range(1, groups):
            send_hv(l, i).start()
        own_out(l).start()

    for l in range(layers):
        absorb(l)
    forward_z(0)
    suffix(0)
    forward_y(0)
    for l in range(1, layers):
        forward_z(l)
        suffix(l)
        forward_y(l)
    for cp in c_po:
        cp.wait()
    for l in range(layers):
        gather_c(l)
        prefix(l)
    for l in range(layers):
        expand(l)

    for l in range(layers):
        own_out(l).wait()
        for i in range(1, groups):
            recv_hv(l, i).wait_recv()
    for l in range(layers):
        for i in range(1, groups):
            send_q(l, i).wait_send()
            send_ql(l, i).wait_send()
            send_lo(l, i).wait_send()
            send_hv(l, i).wait_send()

        def last_z(i):
            for kind in range(2):
                send_z(l, kind, i).wait_send()

        def last_y(i):
            for kind in range(2):
                send_y(l, kind, for_z(i), own_piece(l, kind)).wait_send()

        def last_c(slot):
            for kind in range(2):
                send_c(l, kind, slot).wait_send()

        loop(1, outer, last_z)
        loop(0, outer, last_y)
        others(last_c)


def on_device(mesh, *args):
    qn, qr, ku, vu, pool_lat, pool_rope, table, suf_lat, suf_rope, lengths = args
    layers, seqs, _ = qn.shape
    groups = mesh.shape["dp"]
    ring = mesh.shape["head"]
    heads_dev, rank = ku.shape[1], ku.shape[3]
    per, blk = pool_lat.shape[1], pool_lat.shape[2]
    suf = suf_lat.shape[2]
    nblk = table.shape[1]
    chunk = max(c for c in range(1, 7) if nblk % c == 0)
    rows_g = seqs * heads_dev
    rows = groups * rows_g
    slots = per * ring
    outer = ring // 2
    dims = (layers, seqs, groups, heads_dev, rank, blk, suf, per, ring, nblk, chunk)
    V = pltpu.VMEM
    D = pltpu.SemaphoreType.DMA
    scratch = [
        V(qr.shape, BF16), V(ku.shape, BF16), V(vu.shape, BF16), V(suf_lat.shape, BF16), V(suf_rope.shape, BF16),
        *[V((slots, blk, rank), BF16) for _ in range(layers)],
        *[V((slots, ROPE, blk), BF16) for _ in range(layers)],
        V((layers, groups, seqs, heads_dev * NOPE), BF16),
        V((rank // 128, rows, 128), F32),
        V((layers, groups, rows_g, rank), BF16),
        V((layers, groups, rows_g, rank), BF16),
        V((rows, 128), F32),
        V((layers, rows, 128), BF16),
        V((layers, rows, 1), F32),
        V((layers, rows, 1), F32),
        V((layers, rows, rank), F32),
        V((rows, chunk * blk), F32),
        V((chunk * blk, rank), BF16),
        V((ROPE, chunk * blk), BF16),
        V((layers, groups, rows_g, rank), BF16),
        V((layers, groups, rows_g, rank), BF16),
        V((layers, groups, seqs, heads_dev * VDIM), BF16),
        D((5, layers)), D((2, layers)), D((2, layers)),
        *[D((layers, groups)) for _ in range(8)],
        *[D((layers, 2, outer)) for _ in range(4)],
        *[D((layers, 2, ring)) for _ in range(2)],
    ]
    hbm = pl.BlockSpec(memory_space=pl.ANY)
    smem = pl.BlockSpec(memory_space=pltpu.SMEM)
    return pl.pallas_call(
        functools.partial(kernel, dims),
        out_shape=jax.ShapeDtypeStruct((layers, seqs, HEADS * VDIM), BF16),
        in_specs=[hbm] * 6 + [smem] + [hbm] * 2 + [smem],
        out_specs=hbm,
        scratch_shapes=scratch,
        compiler_params=pltpu.CompilerParams(
            collective_id=0, has_side_effects=True, vmem_limit_bytes=60 * 1024 * 1024
        ),
        name="latent_attention",
    )(*args)


def solution(mesh):
    return jax.shard_map(
        functools.partial(on_device, mesh),
        mesh=mesh,
        in_specs=(
            P(None, ("dp", "head"), None),
            P(None, ("dp", "head"), None),
            P(None, "dp", None, None),
            P(None, "dp", None, None),
            P(None, "head", None, None),
            P(None, "head", None, None),
            P(),
            P(None, ("dp", "head"), None, None),
            P(None, ("dp", "head"), None, None),
            P(("dp", "head")),
        ),
        out_specs=P(None, ("dp", "head"), None),
        check_vma=False,
    )
```

time: 162 us -> 41.3 us (0.25)
  the two profiles are of different devices: /device:TPU:0 before, /device:TPU:9 now
where the time goes in v1:
time: 41.3 us; the launch traced here: 41.2 us
  Pallas kernels  39.6 us (96%)
  local copies, waits for them, and re-layouts  1.57 us (4%)
    pallas_call x1, Pallas kernels, on_device(): pl.pallas_call(functools.partial(kernel, dims), out_shape=jax.ShapeDtypeS...  39.6 us
    unnamed x1, local copies, waits for them, and re-layouts  1.57 us

profile of v1, /device:TPU:9, one launch (start us, length us, event | category | flops | bytes accessed | tf_op | source)
XLA Modules:
  0.0 41.2 jit_solution(5027053883510638313)
XLA Ops:
  0.0 39.6 %latent_attention.1 = bf16[2,16,2048]{2,1,0:T(8,128)(2,1)} custom-call(bf16[2,16,2048]{2,1,0:T(8,128)(2,1)} %refs_0_.1, bf16[2,16,1024]{2,1,0:T(8,128)(2,1)} %refs_1_.1, bf16[2,4,128,512]{3,2,1,0:T(8,128)(2,1)} %refs_2_.1, bf16[2,4,512,128]{3,2,1,0:T(8,128)(2,1)} %refs_3_.1, bf16[2,1,128,512]{3,2,1,0:T(8,128)(2,1)} %refs_4_.1, ...), custom_call_target="tpu_custom_call" | custom-call | tf_op jit(solution)/shard_map/latent_attention/pallas_call | solution.py:435
  39.6 1.6 %copy.12 = bf16[2,16,2048]{2,1,0:T(8,128)(2,1)} copy(bf16[2,16,2048]{2,1,0:T(8,128)(2,1)} %latent_attention.1) | data formatting | bytes 262144

commit v2 on v1

--- a/solution.py
+++ b/solution.py
@@ -89,15 +89,12 @@
 
     for i in range(1, groups):
         greet(lax.rem(dp + i, groups), hd)
-    for_z = lambda i: lax.rem(za + i, outer)
-
-    def greet_z(i, carry):
-        greet(dp, for_z(i) * 2 + yb)
-        return carry
-
-    lax.fori_loop(1, outer, greet_z, 0)
+    has = (za > 0, za < outer - 1)
+    for side in range(2):
+        pl.when(has[side])(lambda: greet(dp, (za + 2 * side - 1) * 2 + yb))
     greet(dp, za * 2 + 1 - yb)
-    pl.semaphore_wait(barrier, (groups - 1) + (outer - 1) + 1)
+    sides = (za + outer - 1) // outer + (2 * outer - 2 - za) // outer
+    pl.semaphore_wait(barrier, groups + sides)
 
     def remote(src, dst, ss, rs, d, h):
         return pltpu.make_async_remote_copy(
@@ -154,18 +151,16 @@
     def own_piece(l, kind):
         return (pool_lat if kind == 0 else pool_rope).at[l, :, half(kind, core)]
 
-    def send_z(l, kind, i):
-        to = for_z(i)
+    def send_z(l, kind, side, a, src):
         return remote(
-            own_piece(l, kind), pool_at(l, kind, hd, core),
-            z_ss.at[l, kind, to], z_rs.at[l, kind, za], dp, to * 2 + yb,
-        )
-
-    def recv_z(l, kind, i):
-        frm = for_z(i)
+            src, pool_at(l, kind, a * 2 + yb, core),
+            z_ss.at[l, kind, side, a], z_rs.at[l, kind, a], dp, (za + 2 * side - 1) * 2 + yb,
+        )
+
+    def recv_z(l, kind, side, a):
         return remote(
-            own_piece(l, kind), pool_at(l, kind, frm * 2 + yb, core),
-            z_ss.at[l, kind, frm], z_rs.at[l, kind, frm], dp, frm * 2 + yb,
+            own_piece(l, kind), pool_at(l, kind, a * 2 + yb, core),
+            z_ss.at[l, kind, side, a], z_rs.at[l, kind, a], dp, (za + 2 * side - 1) * 2 + yb,
         )
 
     def send_y(l, kind, a, src):
@@ -201,31 +196,50 @@
     for l in range(layers):
         for kind in range(2):
             send_y(l, kind, za, own_piece(l, kind)).start()
-
-        def first(i):
-            for kind in range(2):
-                send_z(l, kind, i).start()
-
-        loop(1, outer, first)
-
-    def forward_z(l):
+            for side in range(2):
+                pl.when(has[side])(lambda: send_z(l, kind, side, za, own_piece(l, kind)).start())
+
+    def at_step(i, side):
+        a = za + (2 * side - 1) * i
+        return a, (a >= 0 if side == 0 else a < outer)
+
+    def span(low, high, body):
+        if high - low == 1:
+            body(low)
+        else:
+            loop(low, high, body)
+
+    def forward_z(l, low, high):
         def body(i):
-            for kind in range(2):
-                recv_z(l, kind, i).wait_recv()
-                a = for_z(i)
-                send_y(l, kind, a, pool_at(l, kind, a * 2 + yb, core)).start()
-                send_c(l, kind, a * 2 + yb).start()
-
-        loop(1, outer, body)
-
-    def forward_y(l):
+            for side in range(2):
+                a, there = at_step(i, side)
+
+                @pl.when(there)
+                def _():
+                    for kind in range(2):
+                        recv_z(l, kind, side, a).wait_recv()
+                        piece = pool_at(l, kind, a * 2 + yb, core)
+                        pl.when(has[1 - side])(lambda: send_z(l, kind, 1 - side, a, piece).start())
+                        send_y(l, kind, a, piece).start()
+                        send_c(l, kind, a * 2 + yb).start()
+
+        span(low, high, body)
+
+    def pass_y(l, a):
+        for kind in range(2):
+            recv_y(l, kind, a).wait_recv()
+            send_c(l, kind, a * 2 + 1 - yb).start()
+
+    def forward_y(l, low, high):
         def body(i):
-            for kind in range(2):
-                a = for_z(i)
-                recv_y(l, kind, a).wait_recv()
-                send_c(l, kind, a * 2 + 1 - yb).start()
-
-        loop(0, outer, body)
+            for side in range(2):
+                a, there = at_step(i, side)
+                pl.when(there)(lambda: pass_y(l, a))
+
+        if low == 0:
+            pass_y(l, za)
+        else:
+            span(low, high, body)
 
     def others(body):
         loop(1, ring, lambda i: body(lax.rem(hd + i, ring)))
@@ -344,18 +358,26 @@
             send_hv(l, i).start()
         own_out(l).start()
 
+    mid = outer // 2 + 1
     for l in range(layers):
         absorb(l)
-    forward_z(0)
-    suffix(0)
-    forward_y(0)
-    for l in range(1, layers):
-        forward_z(l)
-        suffix(l)
-        forward_y(l)
-    for cp in c_po:
-        cp.wait()
-    for l in range(layers):
+    for l in range(layers):
+        forward_z(l, 1, 2)
+        forward_y(l, 0, 1)
+    for l in range(layers):
+        forward_z(l, 2, mid)
+        forward_y(l, 1, 2)
+        if l == 0:
+            suffix(l)
+    for l in range(layers):
+        forward_z(l, mid, outer)
+        forward_y(l, 2, mid)
+        forward_y(l, mid, outer)
+        if l > 0:
+            suffix(l)
+        else:
+            for cp in c_po:
+                cp.wait()
         gather_c(l)
         prefix(l)
     for l in range(layers):
@@ -373,12 +395,25 @@
             send_hv(l, i).wait_send()
 
         def last_z(i):
+            for side in range(2):
+                a, there = at_step(i, side)
+                to = 1 - side
+
+                @pl.when(there & has[to])
+                def _():
+                    for kind in range(2):
+                        send_z(l, kind, to, a, own_piece(l, kind)).wait_send()
+
+        def last_y(a):
             for kind in range(2):
-                send_z(l, kind, i).wait_send()
-
-        def last_y(i):
-            for kind in range(2):
-                send_y(l, kind, for_z(i), own_piece(l, kind)).wait_send()
+                send_y(l, kind, a, own_piece(l, kind)).wait_send()
+
+        for side in range(2):
+
+            @pl.when(has[side])
+            def _():
+                for kind in range(2):
+                    send_z(l, kind, side, za, own_piece(l, kind)).wait_send()
 
         def last_c(slot):
             for kind in range(2):
@@ -427,7 +462,8 @@
         V((layers, groups, seqs, heads_dev * VDIM), BF16),
         D((5, layers)), D((2, layers)), D((2, layers)),
         *[D((layers, groups)) for _ in range(8)],
-        *[D((layers, 2, outer)) for _ in range(4)],
+        D((layers, 2, 2, outer)),
+        *[D((layers, 2, outer)) for _ in range(3)],
         *[D((layers, 2, ring)) for _ in range(2)],
     ]
     hbm = pl.BlockSpec(memory_space=pl.ANY)

time: 41.3 us -> 40.4 us (0.978)
  the two profiles are of different devices: /device:TPU:9 before, /device:TPU:0 now
where the time goes in v2:
time: 40.4 us; the launch traced here: 40.2 us
  Pallas kernels  38.7 us (96%)
  local copies, waits for them, and re-layouts  1.57 us (4%)
    pallas_call x1, Pallas kernels, on_device(): pl.pallas_call(functools.partial(kernel, dims), out_shape=jax.ShapeDtypeS...  38.7 us
    unnamed x1, local copies, waits for them, and re-layouts  1.57 us

profile of v2, /device:TPU:0, one launch (start us, length us, event | category | flops | bytes accessed | tf_op | source)
XLA Modules:
  0.0 40.2 jit_solution(2641845667241352293)
XLA Ops:
  0.0 38.7 %latent_attention.1 = bf16[2,16,2048]{2,1,0:T(8,128)(2,1)} custom-call(bf16[2,16,2048]{2,1,0:T(8,128)(2,1)} %refs_0_.1, bf16[2,16,1024]{2,1,0:T(8,128)(2,1)} %refs_1_.1, bf16[2,4,128,512]{3,2,1,0:T(8,128)(2,1)} %refs_2_.1, bf16[2,4,512,128]{3,2,1,0:T(8,128)(2,1)} %refs_3_.1, bf16[2,1,128,512]{3,2,1,0:T(8,128)(2,1)} %refs_4_.1, ...), custom_call_target="tpu_custom_call" | custom-call | tf_op jit(solution)/shard_map/latent_attention/pallas_call | solution.py:471
  38.7 1.6 %copy.12 = bf16[2,16,2048]{2,1,0:T(8,128)(2,1)} copy(bf16[2,16,2048]{2,1,0:T(8,128)(2,1)} %latent_attention.1) | data formatting | bytes 262144

commit v3 on v2

--- a/solution.py
+++ b/solution.py
@@ -38,12 +38,13 @@
     qr_v, ku_v, vu_v, sl_v, sr_v = take(5)
     plat = take(layers)
     prope = take(layers)
-    hq, scr, qls, qlat, qrf, qrot, m_ref, l_ref, acc, s_ref, kbuf, rbuf, los, lr, hvs = take(15)
+    hq, hr, scr, qls, qlat, qrf, qrot, hrot, m_ref, l_ref, acc, s_ref, kbuf, rbuf = take(14)
+    los, lr, sts, strs, hvs = take(5)
     (
         loc_sem, pown_sem, own_sem,
-        q_ss, q_rs, ql_ss, ql_rs, lo_ss, lo_rs, hv_ss, hv_rs,
+        q_ss, q_rs, r_ss, r_rs, st_ss, st_rs, ql_ss, ql_rs, lo_ss, lo_rs, hv_ss, hv_rs,
         z_ss, z_rs, y_ss, y_rs, c_ss, c_rs,
-    ) = take(17)
+    ) = take(21)
 
     dp = lax.axis_index("dp")
     hd = lax.axis_index("head")
@@ -51,7 +52,7 @@
     partner = dp + 1 - 2 * core
     za, yb = hd // 2, lax.rem(hd, 2)
     outer = ring // 2
-    wide = heads_dev * NOPE
+    wide, wide_r = heads_dev * NOPE, heads_dev * ROPE
     rows_g = seqs * heads_dev
     rows = groups * rows_g
     quad = 16 // heads_dev
@@ -69,8 +70,14 @@
             qn.at[l, :, pl.ds(pl.multiple_of(dp * wide, 128), wide)], hq.at[l, dp], own_sem.at[0, l]
         )
 
+    def own_r(l):
+        return pltpu.make_async_copy(
+            qr.at[l, :, pl.ds(pl.multiple_of(dp * wide_r, 128), wide_r)], hr.at[l, dp], own_sem.at[2, l]
+        )
+
     for l in range(layers):
         own_q(l).start()
+        own_r(l).start()
     c_ku = [fetch(ku.at[l], ku_v.at[l], loc_sem.at[0, l]) for l in range(layers)]
     c_qr = fetch(qr, qr_v, loc_sem.at[1, 0])
     c_sl = [fetch(suf_lat.at[l], sl_v.at[l], loc_sem.at[2, l]) for l in range(layers)]
@@ -115,6 +122,17 @@
         j = peer(i)
         return remote(hq.at[l, j], hq.at[l, j], q_ss.at[l, j], q_rs.at[l, j], j, hd)
 
+    def send_r(l, i):
+        j = peer(i)
+        return remote(
+            qr.at[l, :, pl.ds(pl.multiple_of(j * wide_r, 128), wide_r)], hr.at[l, dp],
+            r_ss.at[l, j], r_rs.at[l, dp], j, hd,
+        )
+
+    def recv_r(l, i):
+        j = peer(i)
+        return remote(hr.at[l, j], hr.at[l, j], r_ss.at[l, j], r_rs.at[l, j], j, hd)
+
     def pair(sends, buf, ss, rs):
         def send(l, i):
             j = peer(i)
@@ -128,6 +146,7 @@
 
     send_ql, recv_ql = pair(qls, qlat, ql_ss, ql_rs)
     send_lo, recv_lo = pair(los, lr, lo_ss, lo_rs)
+    send_st, recv_st = pair(sts, strs, st_ss, st_rs)
 
     def cols(j):
         return pl.ds(pl.multiple_of(j * heads_dev * VDIM, 128), heads_dev * VDIM)
@@ -193,6 +212,7 @@
     for l in range(layers):
         for i in range(1, groups):
             send_q(l, i).start()
+            send_r(l, i).start()
     for l in range(layers):
         for kind in range(2):
             send_y(l, kind, za, own_piece(l, kind)).start()
@@ -251,16 +271,25 @@
 
         others(body)
 
-    c_qr.wait()
-    for l in range(layers):
+    def rotary(part, to):
         for g in range(groups):
             for h in range(heads_dev):
-                at = (g * heads_dev + h) * ROPE
-                piece = qr_v[l, :, (at // 128) * 128 : (at // 128 + 1) * 128].astype(F32)
+                at = h * ROPE
+                piece = part(g, at // 128 * 128).astype(F32)
                 if at % 128:
                     piece = pltpu.roll(piece, 128 - at % 128, 1)
                 qrf[pl.ds(g * rows_g + h, seqs, stride=heads_dev), :] = piece
-        qrot[l] = qrf[...].astype(BF16)
+        to[...] = qrf[...].astype(BF16)
+
+    c_qr.wait()
+    for l in range(layers):
+        rotary(lambda g, at: qr_v[l, :, g * wide_r + at : g * wide_r + at + 128], qrot.at[l])
+
+    def held_rotary(l):
+        own_r(l).wait()
+        for i in range(1, groups):
+            recv_r(l, i).wait_recv()
+        rotary(lambda g, at: hr[l, g, :, at : at + 128], hrot.at[l])
 
     def absorb(l):
         own_q(l).wait()
@@ -303,44 +332,46 @@
             w = jnp.exp(s - top)
             tot = jnp.sum(w, axis=1, keepdims=True)
             o = dot(w.astype(BF16), keys)
+            o = o / tot
+            lse = top + jnp.log(tot)
             for g in range(groups):
-                at = slice(g * rows_g + k * 16, g * rows_g + (k + 1) * 16)
-                m_ref[l, at, :] = top[g * 16 : (g + 1) * 16]
-                l_ref[l, at, :] = tot[g * 16 : (g + 1) * 16]
-                acc[l, at, :] = o[g * 16 : (g + 1) * 16]
+                at = slice(k * 16, (k + 1) * 16)
+                los[l, g, at, :] = o[g * 16 : (g + 1) * 16].astype(BF16)
+                m_ref[l, g * rows_g + k * 16 : g * rows_g + (k + 1) * 16, :] = lse[g * 16 : (g + 1) * 16]
+        for g in range(groups):
+            column = jnp.broadcast_to(m_ref[l, g * rows_g : (g + 1) * rows_g, :], (rows_g, 128))
+            sts[l, g] = jnp.concatenate([column] * (128 // rows_g), axis=0).T[:8]
+        for i in range(1, groups):
+            send_lo(l, i).start()
+            send_st(l, i).start()
+        lr[l, dp] = los[l, dp]
+        strs[l, dp] = sts[l, dp]
 
     def prefix(l):
-        def some(b):
+        def some(b, start):
             for j in range(chunk):
                 slot = table[l, b * chunk + j]
                 kbuf[j * blk : (j + 1) * blk, :] = plat[l][slot]
                 rbuf[:, j * blk : (j + 1) * blk] = prope[l][slot]
-            q = qlat[l].reshape(rows, rank)
-            s_ref[...] = (dot_nt(q, kbuf[...]) + dot(qrot[l][:, :ROPE], rbuf[...])) * SCALE
-            old = m_ref[l]
-            top = jnp.maximum(old, jnp.max(s_ref[...], axis=1, keepdims=True))
+            q = qls[l].reshape(rows, rank)
+            s_ref[...] = (dot_nt(q, kbuf[...]) + dot(hrot[l][:, :ROPE], rbuf[...])) * SCALE
+            top = jnp.max(s_ref[...], axis=1, keepdims=True)
+            if not start:
+                top = jnp.maximum(m_ref[l], top)
             w = jnp.exp(s_ref[...] - top)
-            fac = jnp.exp(old - top)
-            l_ref[l] = l_ref[l] * fac + jnp.sum(w, axis=1, keepdims=True)
+            tot = jnp.sum(w, axis=1, keepdims=True)
+            o = dot(w.astype(BF16), kbuf[...])
+            if not start:
+                fac = jnp.exp(m_ref[l] - top)
+                tot = l_ref[l] * fac + tot
+                o = acc[l] * fac + o
+            l_ref[l] = tot
             m_ref[l] = top
-            acc[l] = acc[l] * fac + dot(w.astype(BF16), kbuf[...])
-
-        if nblk == chunk:
-            some(0)
-        else:
-            loop(0, nblk // chunk, some)
-        res = acc[l] / l_ref[l]
-        for c in range(rank // 128):
-            scr[c] = res[:, c * 128 : (c + 1) * 128]
-        for g in range(groups):
-            for h in range(heads_dev):
-                for c in range(rank // 128):
-                    los[l, g, h * seqs : (h + 1) * seqs, c * 128 : (c + 1) * 128] = scr[
-                        c, pl.ds(g * rows_g + h, seqs, stride=heads_dev), :
-                    ].astype(BF16)
-        for i in range(1, groups):
-            send_lo(l, i).start()
-        lr[l, dp] = los[l, dp]
+            acc[l] = o
+
+        some(0, True)
+        if nblk > chunk:
+            loop(1, nblk // chunk, lambda b: some(b, False))
 
     def own_out(l):
         return pltpu.make_async_copy(hvs.at[l, dp], out.at[l, :, cols(dp)], own_sem.at[1, l])
@@ -349,8 +380,21 @@
         c_vu[l].wait()
         for i in range(1, groups):
             recv_lo(l, i).wait_recv()
+            recv_st(l, i).wait_recv()
+        for g in range(groups):
+            at = slice(g * rows_g, (g + 1) * rows_g)
+            lse = jnp.broadcast_to(strs[l, g, 0:1, :], (128, 128)).T[:rows_g, 0:1]
+            old = m_ref[l, at, :]
+            top = jnp.maximum(old, lse)
+            own, pre = jnp.exp(lse - top), jnp.exp(old - top)
+            inv = 1.0 / (own + l_ref[l, at, :] * pre)
+            res = lr[l, g].astype(F32) * (own * inv) + acc[l, at, :] * (pre * inv)
+            for c in range(rank // 128):
+                scr[c, at, :] = res[:, c * 128 : (c + 1) * 128]
         for h in range(heads_dev):
-            x = jnp.concatenate([lr[l, g, h * seqs : (h + 1) * seqs, :] for g in range(groups)], axis=0)
+            x = jnp.concatenate(
+                [scr[c, pl.ds(h, groups * seqs, stride=heads_dev), :] for c in range(rank // 128)], axis=1
+            ).astype(BF16)
             v = dot(x, vu_v[l, h]).astype(BF16)
             for g in range(groups):
                 hvs[l, g, :, h * VDIM : (h + 1) * VDIM] = v[g * seqs : (g + 1) * seqs]
@@ -364,6 +408,7 @@
     for l in range(layers):
         forward_z(l, 1, 2)
         forward_y(l, 0, 1)
+        held_rotary(l)
     for l in range(layers):
         forward_z(l, 2, mid)
         forward_y(l, 1, 2)
@@ -372,15 +417,15 @@
     for l in range(layers):
         forward_z(l, mid, outer)
         forward_y(l, 2, mid)
-        forward_y(l, mid, outer)
         if l > 0:
             suffix(l)
-        else:
-            for cp in c_po:
-                cp.wait()
+    for cp in c_po:
+        cp.wait()
+    for l in range(layers):
+        forward_y(l, mid, outer)
+    for l in range(layers):
         gather_c(l)
         prefix(l)
-    for l in range(layers):
         expand(l)
 
     for l in range(layers):
@@ -390,6 +435,8 @@
     for l in range(layers):
         for i in range(1, groups):
             send_q(l, i).wait_send()
+            send_r(l, i).wait_send()
+            send_st(l, i).wait_send()
             send_ql(l, i).wait_send()
             send_lo(l, i).wait_send()
             send_hv(l, i).wait_send()
@@ -446,10 +493,12 @@
         *[V((slots, blk, rank), BF16) for _ in range(layers)],
         *[V((slots, ROPE, blk), BF16) for _ in range(layers)],
         V((layers, groups, seqs, heads_dev * NOPE), BF16),
+        V((layers, groups, seqs, heads_dev * ROPE), BF16),
         V((rank // 128, rows, 128), F32),
         V((layers, groups, rows_g, rank), BF16),
         V((layers, groups, rows_g, rank), BF16),
         V((rows, 128), F32),
+        V((layers, rows, 128), BF16),
         V((layers, rows, 128), BF16),
         V((layers, rows, 1), F32),
         V((layers, rows, 1), F32),
@@ -459,9 +508,11 @@
         V((ROPE, chunk * blk), BF16),
         V((layers, groups, rows_g, rank), BF16),
         V((layers, groups, rows_g, rank), BF16),
+        V((layers, groups, 8, 128), F32),
+        V((layers, groups, 8, 128), F32),
         V((layers, groups, seqs, heads_dev * VDIM), BF16),
-        D((5, layers)), D((2, layers)), D((2, layers)),
-        *[D((layers, groups)) for _ in range(8)],
+        D((5, layers)), D((2, layers)), D((3, layers)),
+        *[D((layers, groups)) for _ in range(12)],
         D((layers, 2, 2, outer)),
         *[D((layers, 2, outer)) for _ in range(3)],
         *[D((layers, 2, ring)) for _ in range(2)],

time: 40.4 us -> 33.6 us (0.83)
  Pallas kernels: 38.7 us -> 31.8 us
    pallas_call x1, Pallas kernels: 38.7 us -> 31.8 us  [on_device(): pl.pallas_call(functools.partial(kernel, dims), out_shape=jax.ShapeDtypeS...]
where the time goes in v3:
time: 33.6 us; the launch traced here: 33.4 us
  Pallas kernels  31.8 us (95%)
  local copies, waits for them, and re-layouts  1.57 us (5%)
    pallas_call x1, Pallas kernels, on_device(): pl.pallas_call(functools.partial(kernel, dims), out_shape=jax.ShapeDtypeS...  31.8 us
    unnamed x1, local copies, waits for them, and re-layouts  1.57 us

profile of v3, /device:TPU:0, one launch (start us, length us, event | category | flops | bytes accessed | tf_op | source)
XLA Modules:
  0.0 33.4 jit_solution(4706905820867983081)
XLA Ops:
  0.0 31.8 %latent_attention.1 = bf16[2,16,2048]{2,1,0:T(8,128)(2,1)} custom-call(bf16[2,16,2048]{2,1,0:T(8,128)(2,1)} %refs_0_.1, bf16[2,16,1024]{2,1,0:T(8,128)(2,1)} %refs_1_.1, bf16[2,4,128,512]{3,2,1,0:T(8,128)(2,1)} %refs_2_.1, bf16[2,4,512,128]{3,2,1,0:T(8,128)(2,1)} %refs_3_.1, bf16[2,1,128,512]{3,2,1,0:T(8,128)(2,1)} %refs_4_.1, ...), custom_call_target="tpu_custom_call" | custom-call | tf_op jit(solution)/shard_map/latent_attention/pallas_call | solution.py:522
  31.8 1.6 %copy.12 = bf16[2,16,2048]{2,1,0:T(8,128)(2,1)} copy(bf16[2,16,2048]{2,1,0:T(8,128)(2,1)} %latent_attention.1) | data formatting | bytes 262144

commit v4 on v3

--- a/solution.py
+++ b/solution.py
@@ -13,6 +13,7 @@
 VDIM = 128
 SCALE = (NOPE + ROPE) ** (-0.5)
 MESH = pl.DeviceIdType.MESH
+KINDS = 3
 F32 = jnp.float32
 BF16 = jnp.bfloat16
 NT = (((1,), (1,)), ((), ()))
@@ -80,14 +81,6 @@
         own_r(l).start()
     c_ku = [fetch(ku.at[l], ku_v.at[l], loc_sem.at[0, l]) for l in range(layers)]
     c_qr = fetch(qr, qr_v, loc_sem.at[1, 0])
-    c_sl = [fetch(suf_lat.at[l], sl_v.at[l], loc_sem.at[2, l]) for l in range(layers)]
-    c_sr = [fetch(suf_rope.at[l], sr_v.at[l], loc_sem.at[3, l]) for l in range(layers)]
-    c_po = []
-    for l in range(layers):
-        mine = pl.ds(hd * per, per)
-        c_po.append(fetch(pool_lat.at[l], plat[l].at[mine], pown_sem.at[0, l]))
-        c_po.append(fetch(pool_rope.at[l], prope[l].at[mine], pown_sem.at[1, l]))
-    c_vu = [fetch(vu.at[l], vu_v.at[l], loc_sem.at[4, l]) for l in range(layers)]
 
     barrier = pltpu.get_barrier_semaphore()
 
@@ -160,15 +153,17 @@
         return remote(hvs.at[l, j], out.at[l, :, cols(j)], hv_ss.at[l, j], hv_rs.at[l, j], j, hd)
 
     def half(kind, c):
-        size = (blk if kind == 0 else ROPE) // 2
-        return pl.ds(pl.multiple_of(c * size, 16), size)
+        parts = KINDS - 1 if kind < KINDS - 1 else 1
+        size = (blk if kind < KINDS - 1 else ROPE) // 2 // parts
+        at = (c * parts + (kind if kind < KINDS - 1 else 0)) * size
+        return pl.ds(pl.multiple_of(at, 16), size)
 
     def pool_at(l, kind, slot, c):
-        buf = (plat if kind == 0 else prope)[l]
+        buf = (plat if kind < KINDS - 1 else prope)[l]
         return buf.at[pl.ds(slot * per, per), half(kind, c)]
 
     def own_piece(l, kind):
-        return (pool_lat if kind == 0 else pool_rope).at[l, :, half(kind, core)]
+        return (pool_lat if kind < KINDS - 1 else pool_rope).at[l, :, half(kind, core)]
 
     def send_z(l, kind, side, a, src):
         return remote(
@@ -214,10 +209,19 @@
             send_q(l, i).start()
             send_r(l, i).start()
     for l in range(layers):
-        for kind in range(2):
+        for kind in range(KINDS):
             send_y(l, kind, za, own_piece(l, kind)).start()
             for side in range(2):
                 pl.when(has[side])(lambda: send_z(l, kind, side, za, own_piece(l, kind)).start())
+
+    c_sl = [fetch(suf_lat.at[l], sl_v.at[l], loc_sem.at[2, l]) for l in range(layers)]
+    c_sr = [fetch(suf_rope.at[l], sr_v.at[l], loc_sem.at[3, l]) for l in range(layers)]
+    c_po = []
+    for l in range(layers):
+        mine = pl.ds(hd * per, per)
+        c_po.append(fetch(pool_lat.at[l], plat[l].at[mine], pown_sem.at[0, l]))
+        c_po.append(fetch(pool_rope.at[l], prope[l].at[mine], pown_sem.at[1, l]))
+    c_vu = [fetch(vu.at[l], vu_v.at[l], loc_sem.at[4, l]) for l in range(layers)]
 
     def at_step(i, side):
         a = za + (2 * side - 1) * i
@@ -236,7 +240,7 @@
 
                 @pl.when(there)
                 def _():
-                    for kind in range(2):
+                    for kind in range(KINDS):
                         recv_z(l, kind, side, a).wait_recv()
                         piece = pool_at(l, kind, a * 2 + yb, core)
                         pl.when(has[1 - side])(lambda: send_z(l, kind, 1 - side, a, piece).start())
@@ -246,7 +250,7 @@
         span(low, high, body)
 
     def pass_y(l, a):
-        for kind in range(2):
+        for kind in range(KINDS):
             recv_y(l, kind, a).wait_recv()
             send_c(l, kind, a * 2 + 1 - yb).start()
 
@@ -266,7 +270,7 @@
 
     def gather_c(l):
         def body(slot):
-            for kind in range(2):
+            for kind in range(KINDS):
                 recv_c(l, kind, slot).wait_recv()
 
         others(body)
@@ -448,22 +452,22 @@
 
                 @pl.when(there & has[to])
                 def _():
-                    for kind in range(2):
+                    for kind in range(KINDS):
                         send_z(l, kind, to, a, own_piece(l, kind)).wait_send()
 
         def last_y(a):
-            for kind in range(2):
+            for kind in range(KINDS):
                 send_y(l, kind, a, own_piece(l, kind)).wait_send()
 
         for side in range(2):
 
             @pl.when(has[side])
             def _():
-                for kind in range(2):
+                for kind in range(KINDS):
                     send_z(l, kind, side, za, own_piece(l, kind)).wait_send()
 
         def last_c(slot):
-            for kind in range(2):
+            for kind in range(KINDS):
                 send_c(l, kind, slot).wait_send()
 
         loop(1, outer, last_z)
@@ -513,9 +517,9 @@
         V((layers, groups, seqs, heads_dev * VDIM), BF16),
         D((5, layers)), D((2, layers)), D((3, layers)),
         *[D((layers, groups)) for _ in range(12)],
-        D((layers, 2, 2, outer)),
-        *[D((layers, 2, outer)) for _ in range(3)],
-        *[D((layers, 2, ring)) for _ in range(2)],
+        D((layers, KINDS, 2, outer)),
+        *[D((layers, KINDS, outer)) for _ in range(3)],
+        *[D((layers, KINDS, ring)) for _ in range(2)],
     ]
     hbm = pl.BlockSpec(memory_space=pl.ANY)
     smem = pl.BlockSpec(memory_space=pltpu.SMEM)

time: 33.6 us -> 34.2 us (1.018)
  Pallas kernels: 31.8 us -> 32.5 us
    pallas_call x1, Pallas kernels: 31.8 us -> 32.5 us  [on_device(): pl.pallas_call(functools.partial(kernel, dims), out_shape=jax.ShapeDtypeS...]
where the time goes in v4:
time: 34.2 us; the launch traced here: 34 us
  Pallas kernels  32.5 us (95%)
  local copies, waits for them, and re-layouts  1.57 us (5%)
    pallas_call x1, Pallas kernels, on_device(): pl.pallas_call(functools.partial(kernel, dims), out_shape=jax.ShapeDtypeS...  32.5 us
    unnamed x1, local copies, waits for them, and re-layouts  1.57 us

profile of v4, /device:TPU:0, one launch (start us, length us, event | category | flops | bytes accessed | tf_op | source)
XLA Modules:
  0.0 34.0 jit_solution(12629280440106427321)
XLA Ops:
  0.0 32.5 %latent_attention.1 = bf16[2,16,2048]{2,1,0:T(8,128)(2,1)} custom-call(bf16[2,16,2048]{2,1,0:T(8,128)(2,1)} %refs_0_.1, bf16[2,16,1024]{2,1,0:T(8,128)(2,1)} %refs_1_.1, bf16[2,4,128,512]{3,2,1,0:T(8,128)(2,1)} %refs_2_.1, bf16[2,4,512,128]{3,2,1,0:T(8,128)(2,1)} %refs_3_.1, bf16[2,1,128,512]{3,2,1,0:T(8,128)(2,1)} %refs_4_.1, ...), custom_call_target="tpu_custom_call" | custom-call | tf_op jit(solution)/shard_map/latent_attention/pallas_call | solution.py:526
  32.5 1.6 %copy.12 = bf16[2,16,2048]{2,1,0:T(8,128)(2,1)} copy(bf16[2,16,2048]{2,1,0:T(8,128)(2,1)} %latent_attention.1) | data formatting | bytes 262144
